TPU v7x, 256 devices: a whole 4x4x8 slice. The times are simulated.
256 devices in a mesh: cells: 16 (over z, core), lev: 16 (over x, y).
Axes of the slice: x: 4, y: 4, z: 8, core: 2. Of those that a mesh axis runs over, the one named last changes fastest.
Arguments:
- source_levels: float32 [128, 65536], P('lev', 'cells'), may hold values from -6 to 6
- level_to_mode: float32 [128, 128], replicated, may hold values from -0.5 to 0.5
- mode_to_level: float32 [128, 128], replicated, may hold values from -0.5 to 0.5
- mode_shift: float32 [128], P('lev'), may hold values from 0.02 to 1
- edge_weight: float32 [6, 65536], P(None, 'cells'), may hold values from 0.05 to 0.5
- neighbours: int32 [6, 65536], P(None, 'cells'), may hold values from 0 to 6143, as said below
- send_lists: int32 [16, 2048], P('cells'), may hold values from 0 to 4095, as said below
Outputs:
- correction: float32 [128, 65536], P('lev', 'cells')
Inputs may be any that keep to these rules, and one draw needn't show every extreme that they name: `neighbours`: an entry below 4096 is a cell of the same partition whose local index differs from the cell's own local index by at most 32; an entry e of partition p at or above 4096 names halo slot h = (e - 4096) % 128 from partition s = (e - 4096) // 128, with s not p and h below the number of cells that s sends to p. An unused entry names the cell itself. `send_lists`: the number of used slots from partition s to partition q differs from pair to pair: 1 to 128 for every pair of different partitions, 0 for a partition and itself; in every draw some partition receives 128 cells from every other one. Unused slots hold any cell.
All inputs are finite; a program needn't handle non-finite values.
Results may differ from a plain program's by a relative error of at most 0.00007.
Values sent between devices are 32-bit elements; how exact they have to be, the bound alone decides.
A program may use at most 64 MiB of HBM per device.

v0:
```python
import jax
import jax.numpy as jnp
from jax import lax
from jax.sharding import PartitionSpec as P

DEG = 6
HMAX = 128
SWEEPS = 2
STEPS = 4


def full_product(left, right):
    return jnp.dot(left, right, precision=lax.Precision.HIGHEST, preferred_element_type=jnp.float32)


def local(
    source_levels, level_to_mode, mode_to_level, mode_shift, edge_weight, neighbours, send_lists
):
    slab_rows = source_levels.shape[0]
    position = lax.axis_index("lev")
    send_cells = send_lists.reshape(-1)
    slot_total = send_cells.shape[0]
    diagonal = jnp.sum(edge_weight, axis=0)
    own_rows = lax.dynamic_slice_in_dim(level_to_mode, position * slab_rows, slab_rows, 0)
    mode_field = full_product(own_rows, lax.all_gather(source_levels, "lev", axis=0, tiled=True))
    shift_col = mode_shift[:, None]
    own_scale = shift_col + diagonal[None, :]

    def apply_operator(field):
        outgoing = jnp.take(field, send_cells, axis=1)
        arrived = lax.all_to_all(
            outgoing.reshape(slab_rows, -1, HMAX), "cells", split_axis=1, concat_axis=1, tiled=True
        ).reshape(slab_rows, slot_total)
        extended = jnp.concatenate([field, arrived], axis=1)
        running = own_scale * field
        for slot_number in range(DEG):
            running = running - edge_weight[slot_number][None, :] * jnp.take(
                extended, neighbours[slot_number], axis=1
            )
        return running

    radius = DEG / 2.0
    centre = shift_col + radius
    sigma_ratio = centre / radius
    answer = jnp.zeros_like(mode_field)
    remain = mode_field
    direction = jnp.zeros_like(mode_field)
    factor = 1.0 / sigma_ratio
    for sweep_index in range(SWEEPS):
        for step_index in range(STEPS):
            if step_index == 0:
                if sweep_index > 0:
                    remain = remain - apply_operator(direction)
                factor = 1.0 / sigma_ratio
                direction = remain / centre
            else:
                remain = remain - apply_operator(direction)
                newer = 1.0 / (2.0 * sigma_ratio - factor)
                direction = newer * factor * direction + 2.0 * newer / radius * remain
                factor = newer
            answer = answer + direction
    own_columns = lax.dynamic_slice_in_dim(mode_to_level, position * slab_rows, slab_rows, 1)
    return lax.psum_scatter(
        full_product(own_columns, answer), "lev", scatter_dimension=0, tiled=True
    )


def solution(mesh):
    in_specs = (
        P("lev", "cells"),
        P(),
        P(),
        P("lev"),
        P(None, "cells"),
        P(None, "cells"),
        P("cells", None),
    )
    out_specs = P("lev", "cells")
    return jax.shard_map(local, mesh=mesh, in_specs=in_specs, out_specs=out_specs, check_vma=False)
```

profile of v0, /device:TPU:1, one launch (start us, length us, event | category | flops | bytes accessed | tf_op | source)
XLA Modules:
  0.0 1055.3 jit_solution(7952593365196662498)
XLA Ops:
  21.0 41.8 %all-gather.2.cloned.1.call-done = f32[128,4096]{1,0:T(8,128)} async-done(((f32[8,4096]{1,0:T(8,128)}), f32[128,4096]{1,0:T(8,128)}) %all-gather.2.cloned.1.call-update) | async-done | bytes 2097168 | tf_op jit(solution)/shard_map/all_gather | solution.py:25
  93.4 15.4 %gather_fusion.6 = f32[4096,8]{1,0:T(8,128)} fusion(f32[8,6144]{0,1:T(8,128)S(1)} %copy.108, s32[4096]{0:T(1024)} %fusion.90), kind=kCustom, calls=%fused_computation.12.clone | custom fusion | bytes 278528 | tf_op jit(solution)/shard_map/jit(_take)/gather | solution.py:37
  337.2 15.4 %gather_fusion.20 = f32[4096,8]{1,0:T(8,128)} fusion(f32[8,6144]{0,1:T(8,128)S(1)} %copy.136, s32[4096]{0:T(1024)} %fusion.90), kind=kCustom, calls=%fused_computation.24.clone | custom fusion | bytes 278528 | tf_op jit(solution)/shard_map/jit(_take)/gather | solution.py:37
  352.6 15.4 %gather_fusion.19 = f32[4096,8]{1,0:T(8,128)} fusion(f32[8,6144]{0,1:T(8,128)S(1)} %copy.136, s32[4096]{0:T(1024)} %fusion.89), kind=kCustom, calls=%fused_computation.23.clone | custom fusion | bytes 278528 | tf_op jit(solution)/shard_map/jit(_take)/gather | solution.py:37
  368.0 15.4 %gather_fusion.18 = f32[4096,8]{1,0:T(8,128)} fusion(f32[8,6144]{0,1:T(8,128)S(1)} %copy.136, s32[4096]{0:T(1024)} %fusion.88), kind=kCustom, calls=%fused_computation.22.clone | custom fusion | bytes 278528 | tf_op jit(solution)/shard_map/jit(_take)/gather | solution.py:37
  398.9 15.4 %gather_fusion.16 = f32[4096,8]{1,0:T(8,128)} fusion(f32[8,6144]{0,1:T(8,128)S(1)} %copy.136, s32[4096]{0:T(1024)} %fusion.86), kind=kCustom, calls=%fused_computation.20.clone | custom fusion | bytes 278528 | tf_op jit(solution)/shard_map/jit(_take)/gather | solution.py:37
  414.3 15.4 %gather_fusion.15 = f32[4096,8]{1,0:T(8,128)} fusion(f32[8,6144]{0,1:T(8,128)S(1)} %copy.136, s32[4096]{0:T(1024)} %fusion.85), kind=kCustom, calls=%fused_computation.19.clone | custom fusion | bytes 278528 | tf_op jit(solution)/shard_map/jit(_take)/gather | solution.py:37
  465.5 15.4 %gather_fusion.27 = f32[4096,8]{1,0:T(8,128)} fusion(f32[8,6144]{0,1:T(8,128)S(1)} %copy.150, s32[4096]{0:T(1024)} %fusion.90), kind=kCustom, calls=%fused_computation.30.clone | custom fusion | bytes 278528 | tf_op jit(solution)/shard_map/jit(_take)/gather | solution.py:37
  496.3 15.4 %gather_fusion.25 = f32[4096,8]{1,0:T(8,128)} fusion(f32[8,6144]{0,1:T(8,128)S(1)} %copy.150, s32[4096]{0:T(1024)} %fusion.88), kind=kCustom, calls=%fused_computation.28.clone | custom fusion | bytes 278528 | tf_op jit(solution)/shard_map/jit(_take)/gather | solution.py:37
  527.1 15.4 %gather_fusion.23 = f32[4096,8]{1,0:T(8,128)} fusion(f32[8,6144]{0,1:T(8,128)S(1)} %copy.150, s32[4096]{0:T(1024)} %fusion.86), kind=kCustom, calls=%fused_computation.26.clone | custom fusion | bytes 278528 | tf_op jit(solution)/shard_map/jit(_take)/gather | solution.py:37
  542.6 15.4 %gather_fusion.22 = f32[4096,8]{1,0:T(8,128)} fusion(f32[8,6144]{0,1:T(8,128)S(1)} %copy.150, s32[4096]{0:T(1024)} %fusion.85), kind=kCustom, calls=%fused_computation.25.clone | custom fusion | bytes 278528 | tf_op jit(solution)/shard_map/jit(_take)/gather | solution.py:37
  592.7 15.4 %gather_fusion.34 = f32[4096,8]{1,0:T(8,128)} fusion(f32[8,6144]{0,1:T(8,128)S(1)} %copy.164, s32[4096]{0:T(1024)} %fusion.90), kind=kCustom, calls=%fused_computation.36.clone | custom fusion | bytes 278528 | tf_op jit(solution)/shard_map/jit(_take)/gather | solution.py:37
  623.6 15.4 %gather_fusion.32 = f32[4096,8]{1,0:T(8,128)} fusion(f32[8,6144]{0,1:T(8,128)S(1)} %copy.164, s32[4096]{0:T(1024)} %fusion.88), kind=kCustom, calls=%fused_computation.34.clone | custom fusion | bytes 278528 | tf_op jit(solution)/shard_map/jit(_take)/gather | solution.py:37
  654.4 15.4 %gather_fusion.30 = f32[4096,8]{1,0:T(8,128)} fusion(f32[8,6144]{0,1:T(8,128)S(1)} %copy.164, s32[4096]{0:T(1024)} %fusion.86), kind=kCustom, calls=%fused_computation.32.clone | custom fusion | bytes 278528 | tf_op jit(solution)/shard_map/jit(_take)/gather | solution.py:37
  669.8 15.4 %gather_fusion.29 = f32[4096,8]{1,0:T(8,128)} fusion(f32[8,6144]{0,1:T(8,128)S(1)} %copy.164, s32[4096]{0:T(1024)} %fusion.85), kind=kCustom, calls=%fused_computation.31.clone | custom fusion | bytes 278528 | tf_op jit(solution)/shard_map/jit(_take)/gather | solution.py:37
  719.4 15.4 %gather_fusion.41 = f32[4096,8]{1,0:T(8,128)} fusion(f32[8,6144]{0,1:T(8,128)S(1)} %copy.178, s32[4096]{0:T(1024)} %fusion.90), kind=kCustom, calls=%fused_computation.42.clone | custom fusion | bytes 278528 | tf_op jit(solution)/shard_map/jit(_take)/gather | solution.py:37
  750.2 15.4 %gather_fusion.39 = f32[4096,8]{1,0:T(8,128)} fusion(f32[8,6144]{0,1:T(8,128)S(1)} %copy.178, s32[4096]{0:T(1024)} %fusion.88), kind=kCustom, calls=%fused_computation.40.clone | custom fusion | bytes 278528 | tf_op jit(solution)/shard_map/jit(_take)/gather | solution.py:37
  781.1 15.4 %gather_fusion.37 = f32[4096,8]{1,0:T(8,128)} fusion(f32[8,6144]{0,1:T(8,128)S(1)} %copy.178, s32[4096]{0:T(1024)} %fusion.86), kind=kCustom, calls=%fused_computation.38.clone | custom fusion | bytes 278528 | tf_op jit(solution)/shard_map/jit(_take)/gather | solution.py:37
  796.5 15.4 %gather_fusion.36 = f32[4096,8]{1,0:T(8,128)} fusion(f32[8,6144]{0,1:T(8,128)S(1)} %copy.178, s32[4096]{0:T(1024)} %fusion.85), kind=kCustom, calls=%fused_computation.37.clone | custom fusion | bytes 278528 | tf_op jit(solution)/shard_map/jit(_take)/gather | solution.py:37
  846.7 15.4 %gather_fusion.48 = f32[4096,8]{1,0:T(8,128)} fusion(f32[8,6144]{0,1:T(8,128)S(1)} %copy.192, s32[4096]{0:T(1024)} %fusion.90), kind=kCustom, calls=%fused_computation.48.clone | custom fusion | bytes 278528 | tf_op jit(solution)/shard_map/jit(_take)/gather | solution.py:37
  877.6 15.4 %gather_fusion.46 = f32[4096,8]{1,0:T(8,128)} fusion(f32[8,6144]{0,1:T(8,128)S(1)} %copy.192, s32[4096]{0:T(1024)} %fusion.88), kind=kCustom, calls=%fused_computation.46.clone | custom fusion | bytes 278528 | tf_op jit(solution)/shard_map/jit(_take)/gather | solution.py:37
  908.4 15.4 %gather_fusion.44 = f32[4096,8]{1,0:T(8,128)} fusion(f32[8,6144]{0,1:T(8,128)S(1)} %copy.192, s32[4096]{0:T(1024)} %fusion.86), kind=kCustom, calls=%fused_computation.44.clone | custom fusion | bytes 278528 | tf_op jit(solution)/shard_map/jit(_take)/gather | solution.py:37
  923.8 15.4 %gather_fusion.43 = f32[4096,8]{1,0:T(8,128)} fusion(f32[8,6144]{0,1:T(8,128)S(1)} %copy.192, s32[4096]{0:T(1024)} %fusion.85), kind=kCustom, calls=%fused_computation.43.clone | custom fusion | bytes 278528 | tf_op jit(solution)/shard_map/jit(_take)/gather | solution.py:37
  954.5 92.4 %all-reduce.3.cloned.1.call-done = f32[128,4096]{1,0:T(8,128)} async-done(((f32[128,4096]{1,0:T(8,128)}), f32[128,4096]{1,0:T(8,128)}) %all-reduce.3.cloned.1.call-update) | async-done | bytes 2097168
  (422 shorter events, 566.0 us)
Async XLA Ops:
  6.5 943.2 %copy-start = (f32[128,128]{1,0:T(8,128)S(1)}, f32[128,128]{1,0:T(8,128)}, u32[]{:S(2)}) copy-start(f32[128,128]{1,0:T(8,128)} %param.13) | copy-start | bytes 196612
  6.5 56.2 %all-gather.2.cloned.1.call-start = ((), (), s32[]{:S(2)}) async-start(), calls=%async_computation.7 | async-start | bytes 2228224 | tf_op jit(solution)/shard_map/all_gather | solution.py:25
  11.1 54.3 %copy-start.115 = (f32[8]{0:T(128)}, f32[8]{0:T(128)S(1)}, u32[]{:S(2)}) copy-start(f32[8]{0:T(128)S(1)} %get-tuple-element.40) | copy-start | bytes 100
  65.4 130.4 %copy-start.19 = (f32[8,4096]{1,0:T(8,128)}, f32[8,4096]{1,0:T(8,128)S(1)}, u32[]{:S(2)}) copy-start(f32[8,4096]{1,0:T(8,128)S(1)} %get-tuple-element.42) | copy-start | bytes 393220
  72.5 10.5 copy-start.134
  72.5 10.5 copy-start.135
  74.5 16.3 %all-to-all-start = ((f32[8,16,128]{2,0,1:T(8,128)}), f32[8,16,128]{2,0,1:T(8,128)S(1)}, u32[]{:S(2)}, u32[]{:S(2)}) async-start(f32[8,16,128]{2,0,1:T(8,128)} %copy.107), calls=%async_computation | async-start | bytes 131072 | tf_op jit(solution)/shard_map/all_to_all | solution.py:31
  93.4 18.3 %copy-start.49 = (s32[4096]{0:T(1024)S(1)}, s32[4096]{0:T(1024)}, u32[]{:S(2)}) copy-start(s32[4096]{0:T(1024)} %fusion.89) | copy-start | bytes 49156
  111.6 16.9 %copy-start.47 = (s32[4096]{0:T(1024)S(1)}, s32[4096]{0:T(1024)}, u32[]{:S(2)}) copy-start(s32[4096]{0:T(1024)} %fusion.88) | copy-start | bytes 49156
  128.5 16.9 %copy-start.45 = (s32[4096]{0:T(1024)S(1)}, s32[4096]{0:T(1024)}, u32[]{:S(2)}) copy-start(s32[4096]{0:T(1024)} %fusion.87) | copy-start | bytes 49156
  145.4 16.9 %copy-start.41 = (s32[4096]{0:T(1024)S(1)}, s32[4096]{0:T(1024)}, u32[]{:S(2)}) copy-start(s32[4096]{0:T(1024)} %fusion.86) | copy-start | bytes 49156
  162.4 16.9 %copy-start.43 = (s32[4096]{0:T(1024)S(1)}, s32[4096]{0:T(1024)}, u32[]{:S(2)}) copy-start(s32[4096]{0:T(1024)} %fusion.85) | copy-start | bytes 49156
  205.3 13.1 %copy-start.51 = (s32[4096]{0:T(1024)S(1)}, s32[4096]{0:T(1024)}, u32[]{:S(2)}) copy-start(s32[4096]{0:T(1024)} %fusion.90) | copy-start | bytes 49156
  216.5 16.0 %copy-start.50 = (s32[4096]{0:T(1024)S(1)}, s32[4096]{0:T(1024)}, u32[]{:S(2)}) copy-start(s32[4096]{0:T(1024)} %fusion.89) | copy-start | bytes 49156
  216.5 30.1 %copy-start.48 = (s32[4096]{0:T(1024)S(1)}, s32[4096]{0:T(1024)}, u32[]{:S(2)}) copy-start(s32[4096]{0:T(1024)} %fusion.88) | copy-start | bytes 49156
  218.4 42.4 %copy-start.46 = (s32[4096]{0:T(1024)S(1)}, s32[4096]{0:T(1024)}, u32[]{:S(2)}) copy-start(s32[4096]{0:T(1024)} %fusion.87) | copy-start | bytes 49156
  218.4 56.4 %copy-start.42 = (s32[4096]{0:T(1024)S(1)}, s32[4096]{0:T(1024)}, u32[]{:S(2)}) copy-start(s32[4096]{0:T(1024)} %fusion.86) | copy-start | bytes 49156
  232.5 56.4 %copy-start.44 = (s32[4096]{0:T(1024)S(1)}, s32[4096]{0:T(1024)}, u32[]{:S(2)}) copy-start(s32[4096]{0:T(1024)} %fusion.85) | copy-start | bytes 49156
  323.2 11.4 %all-to-all-start.2 = ((f32[8,16,128]{2,0,1:T(8,128)}), f32[8,16,128]{2,0,1:T(8,128)S(1)}, u32[]{:S(2)}, u32[]{:S(2)}) async-start(f32[8,16,128]{2,0,1:T(8,128)} %copy.135), calls=%async_computation.2 | async-start | bytes 131072 | tf_op jit(solution)/shard_map/all_to_all | solution.py:31
  326.8 720.1 %all-reduce.3.cloned.1.call-start = ((), (), s32[]{:S(2)}) async-start(), calls=%async_computation.8 | async-start | bytes 4194304
  442.5 20.4 %copy-start.1 = (f32[8,4096]{1,0:T(8,128)}, f32[8,4096]{1,0:T(8,128)S(1)}, u32[]{:S(2)}) copy-start(f32[8,4096]{1,0:T(8,128)S(1)} %get-tuple-element.13) | copy-start | bytes 393220
  578.5 11.7 %copy-start.26 = (f32[8,4096]{1,0:T(8,128)S(1)}, f32[8,4096]{1,0:T(8,128)}, u32[]{:S(2)}) copy-start(f32[8,4096]{1,0:T(8,128)} %copy-done.25) | copy-start | bytes 393220
  696.5 20.4 %copy-start.4 = (f32[8,4096]{1,0:T(8,128)}, f32[8,4096]{1,0:T(8,128)S(1)}, u32[]{:S(2)}) copy-start(f32[8,4096]{1,0:T(8,128)S(1)} %get-tuple-element.9) | copy-start | bytes 393220
  832.4 11.8 %copy-start.24 = (f32[8,4096]{1,0:T(8,128)S(1)}, f32[8,4096]{1,0:T(8,128)}, u32[]{:S(2)}) copy-start(f32[8,4096]{1,0:T(8,128)} %copy-done.23) | copy-start | bytes 393220
  (119 other events, 431.7 us)
Sparse Core Ops, SparseCore 0:
  9.8 52.8 all-gather.1
  953.3 93.5 all-reduce.2
where the time goes:
time: 1070 us; the launch traced here: 1060 us
  local copies, waits for them, and re-layouts  788 us (74%)
  waiting for transfers between devices  149 us (14%)
  blocking collectives  52 us (5%)
  other arithmetic  32.2 us (3%)
  between operations  15.8 us (1%)
  starting transfers between devices  12.2 us (1%)
    gather x84, local copies, waits for them, and re-layouts, apply_operator(): jnp.take(extended, neighbours[slot_number], axis=1)  712 us
    unnamed x3, waiting for transfers between devices  93.1 us
    all_to_all x5, blocking collectives, apply_operator(): lax.all_to_all(outgoing.reshape(slab_rows, -1, HMAX), 'cells', split_axis...  52 us
    gather x7, local copies, waits for them, and re-layouts, apply_operator(): outgoing = jnp.take(field, send_cells, axis=1)  47.4 us
    all_gather x1, waiting for transfers between devices, local(): lax.all_gather(source_levels, 'lev', axis=0, tiled=True)  41.8 us
  transfers between devices with their start and end apart: 4, of which 4 were waited for; matrix products, arithmetic and copies ran while one was open for 1% of the time, Pallas kernels for 0%

commit v1 on v0

--- a/solution.py
+++ b/solution.py
@@ -2,11 +2,20 @@
 import jax.numpy as jnp
 from jax import lax
 from jax.sharding import PartitionSpec as P
+from jax.lax import axis_index, ppermute, psum
 
 DEG = 6
 HMAX = 128
 SWEEPS = 2
 STEPS = 4
+
+
+def draft_the_view(x_in, at_axis):
+    x_in = jnp.moveaxis(x_in, 0, at_axis)
+    state_now = x_in.shape
+    return x_in.reshape(
+        *state_now[:at_axis], state_now[at_axis] * state_now[at_axis + 1], *state_now[at_axis + 2 :]
+    )
 
 
 def full_product(left, right):
@@ -22,7 +31,23 @@
     slot_total = send_cells.shape[0]
     diagonal = jnp.sum(edge_weight, axis=0)
     own_rows = lax.dynamic_slice_in_dim(level_to_mode, position * slab_rows, slab_rows, 0)
-    mode_field = full_product(own_rows, lax.all_gather(source_levels, "lev", axis=0, tiled=True))
+
+    def ranges_clear(slab_in, axis_name, dim_i):
+        axis_total = psum(1, axis_name)
+        runs = list(map(lambda b: (b, (b + 1) % axis_total), range(axis_total)))
+        pool = [(j, k0) for k0, j in runs]
+        val, f_next = ([], [])
+        for j0 in range(axis_total - 1):
+            if j0 % 2 == 0:
+                val.append(ppermute(val[-1] if val else slab_in, axis_name, runs))
+            else:
+                f_next.append(ppermute(f_next[-1] if f_next else slab_in, axis_name, pool))
+        next_value = jnp.stack([*val[::-1], slab_in, *f_next], axis=0)
+        arr_next = axis_index(axis_name) - len(val)
+        next_value = next_value[(jnp.arange(axis_total) - arr_next) % axis_total]
+        return draft_the_view(next_value, dim_i)
+
+    mode_field = full_product(own_rows, ranges_clear(source_levels, "lev", 0))
     shift_col = mode_shift[:, None]
     own_scale = shift_col + diagonal[None, :]
 

time: 1070 us -> 1100 us (1.028)
  starting transfers between devices: 12.2 us -> 52.7 us
  waiting for transfers between devices: 149 us -> 112 us
  blocking collectives: 52 us -> 63.2 us
  local copies, waits for them, and re-layouts: 788 us -> 799 us
    all_gather x1 -> x0, waiting for transfers between devices: 41.8 us -> none  [local(): lax.all_gather(source_levels, 'lev', axis=0, tiled=True)]
    ppermute x0 -> x15, starting transfers between devices: none -> 35.3 us  [the longest x7 33.1 us: ranges_clear(): f_next.append(ppermute(f_next[-1] if f_next else slab_in, axis_name, pool))]
    ppermute x0 -> x15, waiting for transfers between devices: none -> 15.1 us  [the longest x8 15.1 us: ranges_clear(): val.append(ppermute(val[-1] if val else slab_in, axis_name, runs))]
    all_to_all x5 -> x6, blocking collectives: 52 us -> 63.2 us  [apply_operator(): lax.all_to_all(outgoing.reshape(slab_rows, -1, HMAX), 'cells', split_axis...]
    unnamed x3 -> x2, waiting for transfers between devices: 93.1 us -> 89.5 us
  transfers between devices with their start and end apart: 4 -> 17, of which waited for: 4 -> 9; matrix products, arithmetic and copies ran while one was open for 1% -> 2% of each run, Pallas kernels for 0% -> 0%
where the time goes in v1:
time: 1100 us; the launch traced here: 1080 us
  local copies, waits for them, and re-layouts  799 us (73%)
  waiting for transfers between devices  112 us (10%)
  blocking collectives  63.2 us (6%)
  starting transfers between devices  52.7 us (5%)
  other arithmetic  31.2 us (3%)
  between operations  16.2 us (1%)
    gather x84, local copies, waits for them, and re-layouts, apply_operator(): jnp.take(extended, neighbours[slot_number], axis=1)  712 us
    unnamed x2, waiting for transfers between devices  89.5 us
    all_to_all x6, blocking collectives, apply_operator(): lax.all_to_all(outgoing.reshape(slab_rows, -1, HMAX), 'cells', split_axis...  63.2 us
    gather x7, local copies, waits for them, and re-layouts, apply_operator(): outgoing = jnp.take(field, send_cells, axis=1)  46.4 us
    ppermute x7, starting transfers between devices, ranges_clear(): f_next.append(ppermute(f_next[-1] if f_next else slab_in, axis_name, pool))  33.1 us
  transfers between devices with their start and end apart: 17, of which 9 were waited for; matrix products, arithmetic and copies ran while one was open for 2% of the time, Pallas kernels for 0%

profile of v1, /device:TPU:1, one launch (start us, length us, event | category | flops | bytes accessed | tf_op | source)
XLA Modules:
  0.0 1078.7 jit_solution(5927287248831798010)
XLA Ops:
  93.0 17.4 %all-to-all-start = ((f32[8,16,128]{2,0,1:T(8,128)}), f32[8,16,128]{2,0,1:T(8,128)S(1)}, u32[]{:S(2)}, u32[]{:S(2)}) async-start(f32[8,16,128]{2,0,1:T(8,128)} %copy.107), calls=%async_computation | async-start | bytes 131072 | tf_op jit(solution)/shard_map/all_to_all | solution.py:56
  120.8 15.4 %gather_fusion.7 = f32[4096,8]{1,0:T(8,128)} fusion(f32[8,6144]{0,1:T(8,128)S(1)} %copy.108, s32[4096]{0:T(1024)} %get-tuple-element.49), kind=kCustom, calls=%fused_computation.12.clone | custom fusion | bytes 278528 | tf_op jit(solution)/shard_map/jit(_take)/gather | solution.py:62
  362.4 15.4 %gather_fusion.21 = f32[4096,8]{1,0:T(8,128)} fusion(f32[8,6144]{0,1:T(8,128)S(1)} %copy.136, s32[4096]{0:T(1024)} %get-tuple-element.49), kind=kCustom, calls=%fused_computation.24.clone | custom fusion | bytes 278528 | tf_op jit(solution)/shard_map/jit(_take)/gather | solution.py:62
  393.3 15.4 %gather_fusion.19 = f32[4096,8]{1,0:T(8,128)} fusion(f32[8,6144]{0,1:T(8,128)S(1)} %copy.136, s32[4096]{0:T(1024)} %get-tuple-element.47), kind=kCustom, calls=%fused_computation.22.clone | custom fusion | bytes 278528 | tf_op jit(solution)/shard_map/jit(_take)/gather | solution.py:62
  424.1 15.4 %gather_fusion.17 = f32[4096,8]{1,0:T(8,128)} fusion(f32[8,6144]{0,1:T(8,128)S(1)} %copy.136, s32[4096]{0:T(1024)} %get-tuple-element.45), kind=kCustom, calls=%fused_computation.20.clone | custom fusion | bytes 278528 | tf_op jit(solution)/shard_map/jit(_take)/gather | solution.py:62
  439.5 15.4 %gather_fusion.16 = f32[4096,8]{1,0:T(8,128)} fusion(f32[8,6144]{0,1:T(8,128)S(1)} %copy.136, s32[4096]{0:T(1024)} %get-tuple-element.44), kind=kCustom, calls=%fused_computation.19.clone | custom fusion | bytes 278528 | tf_op jit(solution)/shard_map/jit(_take)/gather | solution.py:62
  490.7 15.4 %gather_fusion.28 = f32[4096,8]{1,0:T(8,128)} fusion(f32[8,6144]{0,1:T(8,128)S(1)} %copy.150, s32[4096]{0:T(1024)} %get-tuple-element.49), kind=kCustom, calls=%fused_computation.30.clone | custom fusion | bytes 278528 | tf_op jit(solution)/shard_map/jit(_take)/gather | solution.py:62
  506.1 15.4 %gather_fusion.27 = f32[4096,8]{1,0:T(8,128)} fusion(f32[8,6144]{0,1:T(8,128)S(1)} %copy.150, s32[4096]{0:T(1024)} %get-tuple-element.48), kind=kCustom, calls=%fused_computation.29.clone | custom fusion | bytes 278528 | tf_op jit(solution)/shard_map/jit(_take)/gather | solution.py:62
  521.5 15.4 %gather_fusion.26 = f32[4096,8]{1,0:T(8,128)} fusion(f32[8,6144]{0,1:T(8,128)S(1)} %copy.150, s32[4096]{0:T(1024)} %get-tuple-element.47), kind=kCustom, calls=%fused_computation.28.clone | custom fusion | bytes 278528 | tf_op jit(solution)/shard_map/jit(_take)/gather | solution.py:62
  552.4 15.4 %gather_fusion.24 = f32[4096,8]{1,0:T(8,128)} fusion(f32[8,6144]{0,1:T(8,128)S(1)} %copy.150, s32[4096]{0:T(1024)} %get-tuple-element.45), kind=kCustom, calls=%fused_computation.26.clone | custom fusion | bytes 278528 | tf_op jit(solution)/shard_map/jit(_take)/gather | solution.py:62
  567.8 15.4 %gather_fusion.23 = f32[4096,8]{1,0:T(8,128)} fusion(f32[8,6144]{0,1:T(8,128)S(1)} %copy.150, s32[4096]{0:T(1024)} %get-tuple-element.44), kind=kCustom, calls=%fused_computation.25.clone | custom fusion | bytes 278528 | tf_op jit(solution)/shard_map/jit(_take)/gather | solution.py:62
  618.2 15.4 %gather_fusion.35 = f32[4096,8]{1,0:T(8,128)} fusion(f32[8,6144]{0,1:T(8,128)S(1)} %copy.164, s32[4096]{0:T(1024)} %get-tuple-element.49), kind=kCustom, calls=%fused_computation.36.clone | custom fusion | bytes 278528 | tf_op jit(solution)/shard_map/jit(_take)/gather | solution.py:62
  649.0 15.4 %gather_fusion.33 = f32[4096,8]{1,0:T(8,128)} fusion(f32[8,6144]{0,1:T(8,128)S(1)} %copy.164, s32[4096]{0:T(1024)} %get-tuple-element.47), kind=kCustom, calls=%fused_computation.34.clone | custom fusion | bytes 278528 | tf_op jit(solution)/shard_map/jit(_take)/gather | solution.py:62
  679.9 15.4 %gather_fusion.31 = f32[4096,8]{1,0:T(8,128)} fusion(f32[8,6144]{0,1:T(8,128)S(1)} %copy.164, s32[4096]{0:T(1024)} %get-tuple-element.45), kind=kCustom, calls=%fused_computation.32.clone | custom fusion | bytes 278528 | tf_op jit(solution)/shard_map/jit(_take)/gather | solution.py:62
  695.3 15.4 %gather_fusion.30 = f32[4096,8]{1,0:T(8,128)} fusion(f32[8,6144]{0,1:T(8,128)S(1)} %copy.164, s32[4096]{0:T(1024)} %get-tuple-element.44), kind=kCustom, calls=%fused_computation.31.clone | custom fusion | bytes 278528 | tf_op jit(solution)/shard_map/jit(_take)/gather | solution.py:62
  744.9 15.4 %gather_fusion.42 = f32[4096,8]{1,0:T(8,128)} fusion(f32[8,6144]{0,1:T(8,128)S(1)} %copy.178, s32[4096]{0:T(1024)} %get-tuple-element.49), kind=kCustom, calls=%fused_computation.42.clone | custom fusion | bytes 278528 | tf_op jit(solution)/shard_map/jit(_take)/gather | solution.py:62
  775.8 15.4 %gather_fusion.40 = f32[4096,8]{1,0:T(8,128)} fusion(f32[8,6144]{0,1:T(8,128)S(1)} %copy.178, s32[4096]{0:T(1024)} %get-tuple-element.47), kind=kCustom, calls=%fused_computation.40.clone | custom fusion | bytes 278528 | tf_op jit(solution)/shard_map/jit(_take)/gather | solution.py:62
  806.6 15.4 %gather_fusion.38 = f32[4096,8]{1,0:T(8,128)} fusion(f32[8,6144]{0,1:T(8,128)S(1)} %copy.178, s32[4096]{0:T(1024)} %get-tuple-element.45), kind=kCustom, calls=%fused_computation.38.clone | custom fusion | bytes 278528 | tf_op jit(solution)/shard_map/jit(_take)/gather | solution.py:62
  822.0 15.4 %gather_fusion.37 = f32[4096,8]{1,0:T(8,128)} fusion(f32[8,6144]{0,1:T(8,128)S(1)} %copy.178, s32[4096]{0:T(1024)} %get-tuple-element.44), kind=kCustom, calls=%fused_computation.37.clone | custom fusion | bytes 278528 | tf_op jit(solution)/shard_map/jit(_take)/gather | solution.py:62
  872.5 15.4 %gather_fusion.49 = f32[4096,8]{1,0:T(8,128)} fusion(f32[8,6144]{0,1:T(8,128)S(1)} %copy.192, s32[4096]{0:T(1024)} %get-tuple-element.49), kind=kCustom, calls=%fused_computation.48.clone | custom fusion | bytes 278528 | tf_op jit(solution)/shard_map/jit(_take)/gather | solution.py:62
  903.3 15.4 %gather_fusion.47 = f32[4096,8]{1,0:T(8,128)} fusion(f32[8,6144]{0,1:T(8,128)S(1)} %copy.192, s32[4096]{0:T(1024)} %get-tuple-element.47), kind=kCustom, calls=%fused_computation.46.clone | custom fusion | bytes 278528 | tf_op jit(solution)/shard_map/jit(_take)/gather | solution.py:62
  934.2 15.4 %gather_fusion.45 = f32[4096,8]{1,0:T(8,128)} fusion(f32[8,6144]{0,1:T(8,128)S(1)} %copy.192, s32[4096]{0:T(1024)} %get-tuple-element.45), kind=kCustom, calls=%fused_computation.44.clone | custom fusion | bytes 278528 | tf_op jit(solution)/shard_map/jit(_take)/gather | solution.py:62
  949.6 15.4 %gather_fusion.44 = f32[4096,8]{1,0:T(8,128)} fusion(f32[8,6144]{0,1:T(8,128)S(1)} %copy.192, s32[4096]{0:T(1024)} %get-tuple-element.44), kind=kCustom, calls=%fused_computation.43.clone | custom fusion | bytes 278528 | tf_op jit(solution)/shard_map/jit(_take)/gather | solution.py:62
  980.2 89.5 %all-reduce.3.cloned.1.call-done = f32[128,4096]{1,0:T(8,128)} async-done(((f32[128,4096]{1,0:T(8,128)}), f32[128,4096]{1,0:T(8,128)}) %all-reduce.3.cloned.1.call-update) | async-done | bytes 2097168
  (437 shorter events, 616.4 us)
Async XLA Ops:
  6.5 969.0 %copy-start = (f32[128,128]{1,0:T(8,128)S(1)}, f32[128,128]{1,0:T(8,128)}, u32[]{:S(2)}) copy-start(f32[128,128]{1,0:T(8,128)} %param.13) | copy-start | bytes 196612
  6.5 68.1 %copy-start.98 = (f32[8,4096]{1,0:T(8,128)S(1)}, f32[8,4096]{1,0:T(8,128)}, u32[]{:S(2)}) copy-start(f32[8,4096]{1,0:T(8,128)} %param.11) | copy-start | bytes 393220
  6.5 11.0 %collective-permute-start = (f32[8,4096]{1,0:T(8,128)}, f32[8,4096]{1,0:T(8,128)S(1)}, u32[]{:S(2)}, u32[]{:S(2)}) collective-permute-start(f32[8,4096]{1,0:T(8,128)} %param.11), channel_id=1, source_target_pairs={{0,1},{1,2},{2,3},{3,4},{4,5},{5,6},{6,7},{7,8},{8,9},{9,10},{10,1... | collective-permute-start | bytes 393224 | tf_op jit(solution)/shard_map/ppermute | solution.py:42
  8.7 16.6 %collective-permute-start.8 = (f32[8,4096]{1,0:T(8,128)}, f32[8,4096]{1,0:T(8,128)S(1)}, u32[]{:S(2)}, u32[]{:S(2)}) collective-permute-start(f32[8,4096]{1,0:T(8,128)} %param.11), channel_id=1, source_target_pairs={{1,0},{2,1},{3,2},{4,3},{5,4},{6,5},{7,6},{8,7},{9,8},{10,9},{11,1... | collective-permute-start | bytes 393224 | tf_op jit(solution)/shard_map/ppermute | solution.py:44
  17.6 7.1 collective-permute-start.1
  24.7 7.1 collective-permute-start.2
  25.3 7.1 collective-permute-start.9
  31.8 7.1 collective-permute-start.3
  32.5 7.8 collective-permute-start.10
  39.0 7.1 collective-permute-start.4
  40.3 7.1 collective-permute-start.11
  46.1 8.1 collective-permute-start.5
  47.4 8.1 collective-permute-start.12
  54.3 8.0 collective-permute-start.6
  55.5 26.7 %copy-start.105 = (f32[8]{0:T(128)}, f32[8]{0:T(128)S(1)}, u32[]{:S(2)}) copy-start(f32[8]{0:T(128)S(1)} %get-tuple-element.40) | copy-start | bytes 100
  55.5 8.3 collective-permute-start.13
  62.3 7.1 collective-permute-start.7
  63.8 15.4 %collective-permute-start.14 = (f32[8,4096]{1,0:T(8,128)S(1)}, f32[8,4096]{1,0:T(8,128)S(1)}, u32[]{:S(2)}, u32[]{:S(2)}) collective-permute-start(f32[8,4096]{1,0:T(8,128)S(1)} %collective-permute-done.13), channel_id=1, source_target_pairs={{1,0},{2,1},{3,2},{4,3},{5,4},{6,5},{7,6},{8,7},{9,8},{10,9},{11,1... | collective-permute-start | bytes 393224 | tf_op jit(solution)/shard_map/ppermute | solution.py:44
  84.0 139.1 %copy-start.19 = (f32[8,4096]{1,0:T(8,128)}, f32[8,4096]{1,0:T(8,128)S(1)}, u32[]{:S(2)}) copy-start(f32[8,4096]{1,0:T(8,128)S(1)} %get-tuple-element.42) | copy-start | bytes 393220
  91.1 19.4 %copy-start.121 = (f32[8]{0:T(128)S(1)}, f32[8]{0:T(128)}, u32[]{:S(2)}) copy-start(f32[8]{0:T(128)} %get-tuple-element.16) | copy-start | bytes 100
  93.0 25.2 %all-to-all-start = ((f32[8,16,128]{2,0,1:T(8,128)}), f32[8,16,128]{2,0,1:T(8,128)S(1)}, u32[]{:S(2)}, u32[]{:S(2)}) async-start(f32[8,16,128]{2,0,1:T(8,128)} %copy.107), calls=%async_computation | async-start | bytes 131072 | tf_op jit(solution)/shard_map/all_to_all | solution.py:56
  110.4 959.3 %all-reduce.3.cloned.1.call-start = ((), (), s32[]{:S(2)}) async-start(), calls=%async_computation.7 | async-start | bytes 4194304
  467.7 20.4 %copy-start.1 = (f32[8,4096]{1,0:T(8,128)}, f32[8,4096]{1,0:T(8,128)S(1)}, u32[]{:S(2)}) copy-start(f32[8,4096]{1,0:T(8,128)S(1)} %get-tuple-element.13) | copy-start | bytes 393220
  721.9 20.4 %copy-start.4 = (f32[8,4096]{1,0:T(8,128)}, f32[8,4096]{1,0:T(8,128)S(1)}, u32[]{:S(2)}) copy-start(f32[8,4096]{1,0:T(8,128)S(1)} %get-tuple-element.9) | copy-start | bytes 393220
  (119 other events, 626.8 us)
Sparse Core Ops, SparseCore 0:
  979.1 90.5 all-reduce.2
